TPU v7x, 32 devices: a whole 2x2x4 slice. The times are simulated.
32 devices in a mesh: dp: 8 (over z, core), tensor: 4 (over y, x).
Axes of the slice: x: 2, y: 2, z: 4, core: 2. Of those that a mesh axis runs over, the one named last changes fastest.
Arguments:
- tokens: bfloat16 [16384, 1152], P(('dp', 'tensor')), may hold values from -6 to 6
- norm_gains: float32 [2, 1152], P(None, ('dp', 'tensor')), may hold values from 0.5 to 1.5
- row_biases: float32 [4, 1152], P(None, ('dp', 'tensor')), may hold values from -3 to 3
- w_qkv: bfloat16 [3, 1152, 1152], P(None, 'dp', 'tensor'), may hold values from -1 to 1
- head_bias: float32 [2, 1152], P(None, 'tensor'), may hold values from -3 to 3
- w_out: bfloat16 [1152, 1152], P('tensor', 'dp'), may hold values from -1.5 to 1.5
- w_fc1: bfloat16 [1152, 4304], P('dp', 'tensor'), may hold values from -0.1875 to 0.1875
- fc1_bias: float32 [4304], P('tensor'), may hold values from -3 to 3
- w_fc2: bfloat16 [4304, 1152], P('tensor', 'dp'), may hold values from -0.09375 to 0.09375
- cotangent: bfloat16 [16384, 1152], P(('dp', 'tensor')), may hold values from -6 to 6
Outputs:
- output: float32 [16384, 1152], P(('dp', 'tensor'))
- grad_tokens: float32 [16384, 1152], P(('dp', 'tensor'))
- grad_norm_gains: float32 [2, 1152], P(None, ('dp', 'tensor'))
- grad_row_biases: float32 [4, 1152], P(None, ('dp', 'tensor'))
- grad_w_qkv: float32 [3, 1152, 1152], P(None, 'dp', 'tensor')
- grad_head_bias: float32 [2, 1152], P(None, 'tensor')
- grad_w_out: float32 [1152, 1152], P('tensor', 'dp')
- grad_w_fc1: float32 [1152, 4304], P('dp', 'tensor')
- grad_fc1_bias: float32 [4304], P('tensor')
- grad_w_fc2: float32 [4304, 1152], P('tensor', 'dp')
All inputs are finite; a program needn't handle non-finite values.
Results may differ from a plain program's by a relative error of at most 0.04.
Values may be sent and summed in bfloat16 or wider, within the bound.
No kernel may reach another device: no remote copies, remote signals or barrier semaphores. Data moves between devices by JAX's collectives and lax.ppermute only.
A program may use at most 192 MiB of HBM per device.

v0:
```python
import jax
import jax.numpy as jnp
from jax import lax
from jax.sharding import PartitionSpec as P

HD = 72
SEQ = 256
EPS = 1e-06


def norm_rows(values, gain_row, shifts):
    center = values - jnp.mean(values, axis=-1, keepdims=True)
    spread = lax.rsqrt(jnp.mean(center * center, axis=-1, keepdims=True) + EPS)
    normed = center * spread
    return (normed * gain_row + shifts, normed, spread)


def norm_back(grad_rows, normed, spread, gain_row):
    scaled = grad_rows * gain_row
    return spread * (
        scaled
        - jnp.mean(scaled, axis=-1, keepdims=True)
        - normed * jnp.mean(scaled * normed, axis=-1, keepdims=True)
    )


def gelu_tanh(pre_act):
    return jax.nn.gelu(pre_act, approximate=True)


def image_block(image_total):
    block_size = min(image_total, max(1, 512 // SEQ))
    while image_total % block_size:
        block_size = block_size - 1
    return block_size


def attend(block_in):
    query_b, keys_b, vals_b = block_in
    scores = jnp.einsum("gqhe,gkhe->ghqk", query_b, keys_b, preferred_element_type=jnp.float32)
    top_score = jnp.max(scores, axis=-1, keepdims=True)
    log_norm = top_score + jnp.log(jnp.sum(jnp.exp(scores - top_score), axis=-1, keepdims=True))
    probs_b = jnp.exp(scores - log_norm).astype(jnp.bfloat16)
    mixed = jnp.einsum(
        "ghqk,gkhe->gqhe", probs_b, vals_b, preferred_element_type=jnp.float32
    ).astype(jnp.bfloat16)
    return (mixed, log_norm[..., 0])


def attend_back(block_in):
    query_b, keys_b, vals_b, grad_b, log_norm = block_in
    scores = jnp.einsum("gqhe,gkhe->ghqk", query_b, keys_b, preferred_element_type=jnp.float32)
    probs_f = jnp.exp(scores - log_norm[..., None])
    probs_b = probs_f.astype(jnp.bfloat16)
    grad_vals = jnp.einsum("ghqk,gqhe->gkhe", probs_b, grad_b, preferred_element_type=jnp.float32)
    grad_probs = jnp.einsum("gqhe,gkhe->ghqk", grad_b, vals_b, preferred_element_type=jnp.float32)
    grad_scores = probs_f * (grad_probs - jnp.sum(probs_f * grad_probs, axis=-1, keepdims=True))
    grad_scores_b = grad_scores.astype(jnp.bfloat16)
    grad_query = jnp.einsum(
        "ghqk,gkhe->gqhe", grad_scores_b, keys_b, preferred_element_type=jnp.float32
    ) * HD ** (-0.5)
    grad_keys = jnp.einsum(
        "ghqk,gqhe->gkhe", grad_scores_b, query_b, preferred_element_type=jnp.float32
    )
    return (grad_query, grad_keys, grad_vals)


def body(
    tokens, norm_gains, row_biases, w_qkv, head_bias, w_out, w_fc1, fc1_bias, w_fc2, cotangent
):
    inv_root = HD ** (-0.5)
    gain_rows, shifts = (
        lax.all_gather(norm_gains, ("dp", "tensor"), axis=1, tiled=True),
        lax.all_gather(row_biases, ("dp", "tensor"), axis=1, tiled=True),
    )
    qkv_full, out_full, fc1_full, fc2_full = (
        lax.all_gather(w_qkv, "dp", axis=1, tiled=True),
        lax.all_gather(w_out, "dp", axis=1, tiled=True),
        lax.all_gather(w_fc1, "dp", axis=0, tiled=True),
        lax.all_gather(w_fc2, "dp", axis=1, tiled=True),
    )
    inputs_f = tokens.astype(jnp.float32)
    first_f, normed_one, spread_one = norm_rows(inputs_f, gain_rows[0], shifts[0])
    first_in, cot_all = (
        lax.all_gather(first_f.astype(jnp.bfloat16), "tensor", axis=0, tiled=True),
        lax.all_gather(cotangent, "tensor", axis=0, tiled=True),
    )
    group_rows = first_in.shape[0]
    images = group_rows // SEQ
    local_width = w_qkv.shape[2]
    local_heads = local_width // HD
    block_size = image_block(images)

    def to_blocks(array_in):
        return array_in.reshape(images // block_size, block_size, SEQ, local_heads, HD)

    query_rows = (
        (jnp.dot(first_in, qkv_full[0], preferred_element_type=jnp.float32) + head_bias[0])
        * inv_root
    ).astype(jnp.bfloat16)
    keys_rows = jnp.dot(first_in, qkv_full[1], preferred_element_type=jnp.float32).astype(
        jnp.bfloat16
    )
    vals_rows = (
        jnp.dot(first_in, qkv_full[2], preferred_element_type=jnp.float32) + head_bias[1]
    ).astype(jnp.bfloat16)
    query_blocks = to_blocks(query_rows)
    keys_blocks = to_blocks(keys_rows)
    vals_blocks = to_blocks(vals_rows)
    mixed_blocks, log_norm = lax.map(attend, (query_blocks, keys_blocks, vals_blocks))
    mixed = mixed_blocks.reshape(group_rows, local_width)
    attention = lax.psum_scatter(
        jnp.dot(mixed, out_full, preferred_element_type=jnp.float32).astype(jnp.bfloat16),
        "tensor",
        scatter_dimension=0,
        tiled=True,
    ).astype(jnp.float32)
    hidden_one = inputs_f + attention + shifts[1]
    second_f, normed_two, spread_two = norm_rows(hidden_one, gain_rows[1], shifts[2])
    second_in = lax.all_gather(second_f.astype(jnp.bfloat16), "tensor", axis=0, tiled=True)
    pre_act = jnp.dot(second_in, fc1_full, preferred_element_type=jnp.float32) + fc1_bias
    act_out, gelu_back = jax.vjp(gelu_tanh, pre_act)
    act_in = act_out.astype(jnp.bfloat16)
    mlp_out = lax.psum_scatter(
        jnp.dot(act_in, fc2_full, preferred_element_type=jnp.float32).astype(jnp.bfloat16),
        "tensor",
        scatter_dimension=0,
        tiled=True,
    ).astype(jnp.float32)
    output = hidden_one + mlp_out + shifts[3]
    cot_f = cotangent.astype(jnp.float32)
    grad_fc2 = jnp.dot(act_in.T, cot_all, preferred_element_type=jnp.float32)
    grad_act = jnp.dot(cot_all, fc2_full.T, preferred_element_type=jnp.float32)
    grad_pre = gelu_back(grad_act)[0]
    grad_fc1_bias = jnp.sum(grad_pre, axis=0)
    grad_pre_in = grad_pre.astype(jnp.bfloat16)
    grad_fc1 = jnp.dot(second_in.T, grad_pre_in, preferred_element_type=jnp.float32)
    grad_second = lax.psum_scatter(
        jnp.dot(grad_pre_in, fc1_full.T, preferred_element_type=jnp.float32).astype(jnp.bfloat16),
        "tensor",
        scatter_dimension=0,
        tiled=True,
    ).astype(jnp.float32)
    gain_two = jnp.sum(grad_second * normed_two, axis=0)
    shift_two = jnp.sum(grad_second, axis=0)
    grad_hidden = cot_f + norm_back(grad_second, normed_two, spread_two, gain_rows[1])
    shift_out = jnp.sum(grad_hidden, axis=0)
    shift_fc2 = jnp.sum(cot_f, axis=0)
    grad_hidden_in = grad_hidden.astype(jnp.bfloat16)
    grad_hidden_all = lax.all_gather(grad_hidden_in, "tensor", axis=0, tiled=True)
    grad_wout = jnp.dot(mixed.T, grad_hidden_all, preferred_element_type=jnp.float32)
    grad_mixed = jnp.dot(grad_hidden_all, out_full.T, preferred_element_type=jnp.float32).astype(
        jnp.bfloat16
    )
    grad_query, grad_keys, grad_vals = lax.map(
        attend_back, (query_blocks, keys_blocks, vals_blocks, to_blocks(grad_mixed), log_norm)
    )
    grad_query = grad_query.reshape(group_rows, local_width)
    grad_keys = grad_keys.reshape(group_rows, local_width)
    grad_vals = grad_vals.reshape(group_rows, local_width)
    grad_head = jnp.stack([jnp.sum(grad_query, axis=0), jnp.sum(grad_vals, axis=0)])
    grad_proj = jnp.stack([grad_query, grad_keys, grad_vals]).astype(jnp.bfloat16)
    grad_qkv = jnp.einsum("rd,irk->idk", first_in, grad_proj, preferred_element_type=jnp.float32)
    grad_first = lax.psum_scatter(
        jnp.einsum("irk,idk->rd", grad_proj, qkv_full, preferred_element_type=jnp.float32).astype(
            jnp.bfloat16
        ),
        "tensor",
        scatter_dimension=0,
        tiled=True,
    ).astype(jnp.float32)
    gain_one = jnp.sum(grad_first * normed_one, axis=0)
    shift_one = jnp.sum(grad_first, axis=0)
    grad_tokens = grad_hidden + norm_back(grad_first, normed_one, spread_one, gain_rows[0])
    grad_head_all, grad_fc1_bias_all = lax.psum((grad_head, grad_fc1_bias), "dp")
    grad_qkv_own, grad_out_own, grad_fc1_own, grad_fc2_own = (
        lax.psum_scatter(
            grad_qkv.astype(jnp.bfloat16), "dp", scatter_dimension=1, tiled=True
        ).astype(jnp.float32),
        lax.psum_scatter(
            grad_wout.astype(jnp.bfloat16), "dp", scatter_dimension=1, tiled=True
        ).astype(jnp.float32),
        lax.psum_scatter(
            grad_fc1.astype(jnp.bfloat16), "dp", scatter_dimension=0, tiled=True
        ).astype(jnp.float32),
        lax.psum_scatter(
            grad_fc2.astype(jnp.bfloat16), "dp", scatter_dimension=1, tiled=True
        ).astype(jnp.float32),
    )
    grad_gains_own, grad_shifts_own = (
        lax.psum_scatter(
            jnp.stack([gain_one, gain_two]), ("dp", "tensor"), scatter_dimension=1, tiled=True
        ),
        lax.psum_scatter(
            jnp.stack([shift_one, shift_out, shift_two, shift_fc2]),
            ("dp", "tensor"),
            scatter_dimension=1,
            tiled=True,
        ),
    )
    return (
        output,
        grad_tokens,
        grad_gains_own,
        grad_shifts_own,
        grad_qkv_own,
        grad_head_all,
        grad_out_own,
        grad_fc1_own,
        grad_fc1_bias_all,
        grad_fc2_own,
    )


def solution(mesh):
    in_specs = (
        P(("dp", "tensor"), None),
        P(None, ("dp", "tensor")),
        P(None, ("dp", "tensor")),
        P(None, "dp", "tensor"),
        P(None, "tensor"),
        P("tensor", "dp"),
        P("dp", "tensor"),
        P("tensor"),
        P("tensor", "dp"),
        P(("dp", "tensor"), None),
    )
    out_specs = (
        P(("dp", "tensor"), None),
        P(("dp", "tensor"), None),
        P(None, ("dp", "tensor")),
        P(None, ("dp", "tensor")),
        P(None, "dp", "tensor"),
        P(None, "tensor"),
        P("tensor", "dp"),
        P("dp", "tensor"),
        P("tensor"),
        P("tensor", "dp"),
    )
    return jax.shard_map(body, mesh=mesh, in_specs=in_specs, out_specs=out_specs, check_vma=False)
```

profile of v0, /device:TPU:0, one launch (start us, length us, event | category | flops | bytes accessed | tf_op | source)
XLA Modules:
  0.0 974.4 jit_solution(12943085000319028319)
XLA Ops:
  8.0 71.1 %all-gather = f32[32,36,2]{1,2,0:T(2,128)S(1)} all-gather(f32[1,36,2]{1,2,0:T(2,128)} %bitcast.180), channel_id=1, replica_groups=mesh['dp'=8,'tensor'=4] {'dp','tensor'}, dimensions={0}, use_global_device_ids=true | all-gather | bytes 9504 | tf_op jit(solution)/shard_map/all_gather | solution.py:73
  79.2 63.9 %all-gather.1 = f32[32,36,4]{1,2,0:T(4,128)S(1)} all-gather(f32[1,36,4]{1,2,0:T(4,128)} %bitcast.179), channel_id=1, replica_groups=mesh['dp'=8,'tensor'=4] {'dp','tensor'}, dimensions={0}, use_global_device_ids=true | all-gather | bytes 19008 | tf_op jit(solution)/shard_map/all_gather | solution.py:74
  148.2 16.7 %all_gather.34 = bf16[288,1152]{0,1:T(8,128)(2,1)} all-gather(bf16[288,144]{0,1:T(8,128)(2,1)S(1)} %copy-done.11), channel_id=1, replica_groups=mesh['dp'=8,'tensor'=4] {'dp'}, dimensions={1}, use_global_device_ids=true | all-gather | bytes 746496 | tf_op jit(solution)/shard_map/all_gather | solution.py:78
  164.8 37.7 %all-gather.10.cloned.1.call-done = bf16[2048,1152]{1,0:T(8,128)(2,1)} async-done(((bf16[512,1152]{1,0:T(8,128)(2,1)}), bf16[2048,1152]{1,0:T(8,128)(2,1)}) %all-gather.10.cloned.1.call-update) | async-done | bytes 4718608 | tf_op jit(solution)/shard_map/all_gather | solution.py:85
  208.6 5.3 fusion.56
  226.1 15.5 %while.26 = (s32[]{:T(128)}, bf16[4,2,256,4,72]{2,1,0,4,3:T(2,128)(2,1)}, f32[4,2,4,256]{3,2,1,0:T(4,128)}, bf16[4,2,256,4,72]{2,4,3,1,0:T(8,128)(2,1)}, bf16[4,...) while((s32[]{:T(128)}, bf16[4,2,256,4,72]{2,1,0,4,3:T(2,128)(2,1)}, ...), condition=%wide.region_5.6_spmd, body=%wide.region_2.5_spmd.sunk | while | flops 153761792 | bytes 8127585 | solution.py:110
  245.8 6.5 convolution_convert_fusion.5
  254.4 55.1 %reduce-scatter.13.cloned.1.call-done = bf16[512,1152]{1,0:T(8,128)(2,1)} async-done(((bf16[2048,1152]{1,0:T(8,128)(2,1)}), bf16[512,1152]{1,0:T(8,128)(2,1)}) %reduce-scatter.13.cloned.1.call-update) | async-done | bytes 1179664 | tf_op jit(solution)/shard_map/reduce_scatter | solution.py:112
  314.3 30.7 %all-gather.18.cloned.1.call-done = bf16[1076,1152]{0,1:T(8,128)(2,1)} async-done(((bf16[1076,144]{0,1:T(8,128)(2,1)}), bf16[1076,1152]{0,1:T(8,128)(2,1)}) %all-gather.18.cloned.1.call-update) | async-done | bytes 2479120 | tf_op jit(solution)/shard_map/all_gather | solution.py:80
  345.0 57.8 %all-gather.20.cloned.1.call-done = bf16[2048,1152]{1,0:T(8,128)(2,1)} async-done(((bf16[512,1152]{1,0:T(8,128)(2,1)}), bf16[2048,1152]{1,0:T(8,128)(2,1)}) %all-gather.20.cloned.1.call-update) | async-done | bytes 4718608 | tf_op jit(solution)/shard_map/all_gather | solution.py:86
  402.8 10.7 %fusion.80 = f32[2048,1076]{0,1:T(8,128)} fusion(bf16[2048,1152]{1,0:T(8,128)(2,1)} %all-gather.20.cloned.1.call-done, bf16[1076,1152]{0,1:T(8,128)(2,1)} %all-gather.18.cloned.1.call-done), kind=kOutput, calls=%fused_computation.147 | convolution fusion | flops 5077204992 | bytes 16012288 | tf_op jit(solution)/shard_map/dot_general | solution.py:133
  413.5 24.8 %all-gather.16.cloned.1.call-done = bf16[1152,1076]{1,0:T(8,128)(2,1)} async-done(((bf16[144,1076]{1,0:T(8,128)(2,1)}), bf16[1152,1076]{1,0:T(8,128)(2,1)}) %all-gather.16.cloned.1.call-update) | async-done | bytes 2479120 | tf_op jit(solution)/shard_map/all_gather | solution.py:79
  438.3 58.5 %all-gather.14.cloned.1.call-done = bf16[2048,1152]{1,0:T(8,128)(2,1)} async-done(((bf16[512,1152]{1,0:T(8,128)(2,1)}), bf16[2048,1152]{1,0:T(8,128)(2,1)}) %all-gather.14.cloned.1.call-update) | async-done | bytes 4718608 | tf_op jit(solution)/shard_map/all_gather | solution.py:120
  496.8 18.4 %fusion.74 = (f32[1076]{0:T(1024)}, bf16[2048,1076]{0,1:T(8,128)(2,1)S(1)}, f32[2048,1076]{0,1:T(8,128)}) fusion(f32[2048,1076]{0,1:T(8,128)} %fusion.80, f32[1076]{0:T(1024)} %param.21, bf16[2048,1152]{1,0:T(8,128)(2,1)} %all-gather.14.cloned.1.call-done, bf16[1152,1076]{1,0:T(8,128)(2,1)} %all-gather.16.cloned.1.call-done), kind=kOutput, calls=%fused_computation.142 | convolution fusion | flops 5125684224 | bytes 29242784 | tf_op jit(solution)/shard_map/dot_general | solution.py:121
  517.2 9.1 convolution_convert_fusion.3
  526.4 13.1 %convolution_convert_fusion.4 = bf16[2048,1152]{1,0:T(8,128)(2,1)} fusion(bf16[1076,1152]{0,1:T(8,128)(2,1)} %all-gather.18.cloned.1.call-done, f32[2048,1076]{0,1:T(8,128)} %get-tuple-element.238), kind=kOutput, calls=%fused_computation.60 | convolution fusion | flops 5099397120 | bytes 16012288 | tf_op jit(solution)/shard_map/dot_general | solution.py:125
  539.5 43.9 %reduce-scatter.17.cloned.1.call-done = bf16[512,1152]{1,0:T(8,128)(2,1)} async-done(((bf16[2048,1152]{1,0:T(8,128)(2,1)}), bf16[512,1152]{1,0:T(8,128)(2,1)}) %reduce-scatter.17.cloned.1.call-update) | async-done | bytes 1179664 | tf_op jit(solution)/shard_map/reduce_scatter | solution.py:138
  587.8 55.7 %reduce-scatter.15.cloned.1.call-done = bf16[512,1152]{1,0:T(8,128)(2,1)} async-done(((bf16[2048,1152]{1,0:T(8,128)(2,1)}), bf16[512,1152]{1,0:T(8,128)(2,1)}) %reduce-scatter.15.cloned.1.call-update) | async-done | bytes 1179664 | tf_op jit(solution)/shard_map/reduce_scatter | solution.py:124
  651.1 13.0 %convolution_convert_fusion.1 = bf16[1076,1152]{0,1:T(8,128)(2,1)} fusion(bf16[2048,1152]{1,0:T(8,128)(2,1)} %all-gather.20.cloned.1.call-done, f32[2048,1076]{0,1:T(8,128)} %get-tuple-element.238), kind=kOutput, calls=%fused_computation.57 | convolution fusion | flops 5098277376 | bytes 16012288 | tf_op jit(solution)/shard_map/dot_general | solution.py:132
  664.5 11.6 %convolution_convert_fusion.2 = bf16[1152,1076]{1,0:T(8,128)(2,1)} fusion(bf16[2048,1152]{1,0:T(8,128)(2,1)} %all-gather.14.cloned.1.call-done, bf16[2048,1076]{0,1:T(8,128)(2,1)} %copy-done.33), kind=kOutput, calls=%fused_computation.58 | convolution fusion | flops 5078444544 | bytes 11604992 | tf_op jit(solution)/shard_map/dot_general | solution.py:137
  676.1 31.8 %all-gather.22.cloned.1.call-done = bf16[2048,1152]{1,0:T(8,128)(2,1)} async-done(((bf16[512,1152]{1,0:T(8,128)(2,1)}), bf16[2048,1152]{1,0:T(8,128)(2,1)}) %all-gather.22.cloned.1.call-update) | async-done | bytes 4718608 | tf_op jit(solution)/shard_map/all_gather | solution.py:150
  708.0 5.1 convolution_convert_fusion.7
  717.5 29.5 %while.27 = (s32[]{:T(128)}, f32[4,2,256,4,72]{2,4,3,1,0:T(8,128)}, bf16[4,2,256,4,72]{2,4,3,1,0:T(8,128)(2,1)}, f32[4,2,256,4,72]{2,4,3,1,0:T(8,128)}, bf16[4,2...) while((s32[]{:T(128)}, f32[4,2,256,4,72]{2,4,3,1,0:T(8,128)}, ...), condition=%wide.region_15.16_spmd, body=%wide.region_13.15_spmd.sunk | while | flops 381302784 | bytes 29633716 | solution.py:155
  746.9 6.0 fusion.78
  763.0 6.4 convolution_convert_fusion.6
  775.5 8.2 fusion.48
  788.7 7.4 reshape.126
  796.2 11.0 %bitcast_convert_fusion = bf16[2048,1152]{1,0:T(8,128)(2,1)} fusion(bf16[3,2048,288]{1,2,0:T(8,128)(2,1)} %constant_dynamic-update-slice_fusion, bf16[3,1152,288]{2,1,0:T(8,128)(2,1)} %all-gather.12.cloned.1.call-done), kind=kOutput, calls=%fused_computation.48 | convolution fusion | flops 4079222784 | bytes 10248192 | tf_op jit(solution)/shard_map/irk,idk->rd/dot_general | solution.py:165
  813.7 28.7 %all-reduce.3 = (f32[2,288]{1,0:T(2,128)}, f32[1076]{0:T(1024)}) all-reduce(f32[2,288]{1,0:T(2,128)S(1)} %pad_maximum_fusion.2, f32[1076]{0:T(1024)S(1)} %copy-done.29), channel_id=1, replica_groups=mesh['dp'=8,'tensor'=4] {'dp'}, use_global_device_ids=true, to_apply=%region_30.31 | all-reduce | flops 1652 | bytes 13216 | tf_op jit(solution)/shard_map/psum | solution.py:175
  844.0 14.2 %reduce-scatter.27.cloned.1.call-done = bf16[144,864]{1,0:T(8,128)(2,1)} async-done(((bf16[1152,864]{1,0:T(8,128)(2,1)}), bf16[144,864]{1,0:T(8,128)(2,1)}) %reduce-scatter.27.cloned.1.call-update) | async-done | bytes 248848
  864.6 51.7 %reduce-scatter.19.cloned.1.call-done = bf16[512,1152]{1,0:T(8,128)(2,1)} async-done(((bf16[2048,1152]{1,0:T(8,128)(2,1)}), bf16[512,1152]{1,0:T(8,128)(2,1)}) %reduce-scatter.19.cloned.1.call-update) | async-done | bytes 1179664 | tf_op jit(solution)/shard_map/reduce_scatter | solution.py:164
  921.2 40.3 %all-reduce.2 = (f32[2,1152]{1,0:T(2,128)}, f32[4,1152]{1,0:T(4,128)}) all-reduce(f32[2,1152]{1,0:T(2,128)} %pad_maximum_fusion.1, f32[4,1152]{1,0:T(4,128)} %pad_maximum_fusion), channel_id=6, replica_groups=mesh['dp'=8,'tensor'=4] {'dp','tensor'}, use_global_device_ids=true, to_apply=%region_21.22.clone | all-reduce | flops 6912 | bytes 55296
  (236 shorter events, 145.1 us)
Async XLA Ops:
  7.2 138.3 %copy-start = (bf16[512,1152]{1,0:T(8,128)(2,1)S(1)}, bf16[512,1152]{1,0:T(8,128)(2,1)}, u32[]{:S(2)}) copy-start(bf16[512,1152]{1,0:T(8,128)(2,1)} %param.14) | copy-start | bytes 3538948
  7.2 157.7 %all-gather.12.cloned.1.call-start = ((), (), s32[]{:S(2)}) async-start(), calls=%async_computation.9 | async-start | bytes 2985984 | tf_op jit(solution)/shard_map/all_gather | solution.py:77
  7.9 194.6 %all-gather.10.cloned.1.call-start = ((), (), s32[]{:S(2)}) async-start(), calls=%async_computation.8 | async-start | bytes 5898240 | tf_op jit(solution)/shard_map/all_gather | solution.py:85
  145.9 56.6 %copy-start.15 = (f32[512]{0:T(512)}, f32[512]{0:T(512)S(1)}, u32[]{:S(2)}) copy-start(f32[512]{0:T(512)S(1)} %add_rsqrt_fusion.1) | copy-start | bytes 6148
  147.5 162.0 %reduce-scatter.13.cloned.1.call-start = ((), (), s32[]{:S(2)}) async-start(), calls=%async_computation.10 | async-start | bytes 5898240 | tf_op jit(solution)/shard_map/reduce_scatter | solution.py:112
  241.6 10.7 %copy-start.2 = (bf16[4,2,256,4,72]{2,4,3,1,0:T(8,128)(2,1)}, bf16[4,2,256,4,72]{2,4,3,1,0:T(8,128)(2,1)S(1)}, u32[]{:S(2)}) copy-start(bf16[4,2,256,4,72]{2,4,3,1,0:T(8,128)(2,1)S(1)} %get-tuple-element.416) | copy-start | bytes 3538948
  252.4 92.6 %all-gather.18.cloned.1.call-start = ((), (), s32[]{:S(2)}) async-start(), calls=%async_computation.13 | async-start | bytes 2985984 | tf_op jit(solution)/shard_map/all_gather | solution.py:80
  252.9 149.8 %all-gather.20.cloned.1.call-start = ((), (), s32[]{:S(2)}) async-start(), calls=%async_computation.15 | async-start | bytes 5898240 | tf_op jit(solution)/shard_map/all_gather | solution.py:86
  253.5 184.7 %all-gather.16.cloned.1.call-start = ((), (), s32[]{:S(2)}) async-start(), calls=%async_computation.12 | async-start | bytes 2985984 | tf_op jit(solution)/shard_map/all_gather | solution.py:79
  254.1 242.7 %all-gather.14.cloned.1.call-start = ((), (), s32[]{:S(2)}) async-start(), calls=%async_computation.11 | async-start | bytes 5898240 | tf_op jit(solution)/shard_map/all_gather | solution.py:120
  314.3 269.2 %reduce-scatter.17.cloned.1.call-start = ((), (), s32[]{:S(2)}) async-start(), calls=%async_computation.16 | async-start | bytes 5898240 | tf_op jit(solution)/shard_map/reduce_scatter | solution.py:138
  496.8 20.4 %copy-start.32 = (bf16[1152,1076]{1,0:T(8,128)(2,1)S(1)}, bf16[1152,1076]{1,0:T(8,128)(2,1)}, u32[]{:S(2)}) copy-start(bf16[1152,1076]{1,0:T(8,128)(2,1)} %all-gather.16.cloned.1.call-done) | copy-start | bytes 7437316
  526.3 117.1 %reduce-scatter.15.cloned.1.call-start = ((), (), s32[]{:S(2)}) async-start(), calls=%async_computation.14 | async-start | bytes 5898240 | tf_op jit(solution)/shard_map/reduce_scatter | solution.py:124
  539.5 168.5 %all-gather.22.cloned.1.call-start = ((), (), s32[]{:S(2)}) async-start(), calls=%async_computation.17 | async-start | bytes 5898240 | tf_op jit(solution)/shard_map/all_gather | solution.py:150
  650.9 156.4 %reduce-scatter.25.cloned.1.call-start = ((), (), s32[]{:S(2)}) async-start(), calls=%async_computation.21 | async-start | bytes 2985984 | tf_op jit(solution)/shard_map/reduce_scatter | solution.py:186
  664.2 145.0 %reduce-scatter.23.cloned.1.call-start = ((), (), s32[]{:S(2)}) async-start(), calls=%async_computation.20 | async-start | bytes 2985984 | tf_op jit(solution)/shard_map/reduce_scatter | solution.py:183
  676.1 31.9 %copy-start.8 = (bf16[288,1152]{0,1:T(8,128)(2,1)S(1)}, bf16[288,1152]{0,1:T(8,128)(2,1)}, u32[]{:S(2)}) copy-start(bf16[288,1152]{0,1:T(8,128)(2,1)} %all_gather.34) | copy-start | bytes 1990660
  676.1 166.3 %reduce-scatter.21.cloned.1.call-start = ((), (), s32[]{:S(2)}) async-start(), calls=%async_computation.19 | async-start | bytes 995328 | tf_op jit(solution)/shard_map/reduce_scatter | solution.py:180
  713.1 4.4 copy-start.3
  769.4 88.8 %reduce-scatter.27.cloned.1.call-start = ((), (), s32[]{:S(2)}) async-start(), calls=%async_computation.22 | async-start | bytes 2322432
  796.2 120.2 %reduce-scatter.19.cloned.1.call-start = ((), (), s32[]{:S(2)}) async-start(), calls=%async_computation.18 | async-start | bytes 5898240 | tf_op jit(solution)/shard_map/reduce_scatter | solution.py:164
  807.2 4.5 copy-start.18
  807.2 5.1 copy-start.22
  807.2 5.7 copy-start.21
  807.2 6.2 copy-start.28
  807.2 6.3 copy-start.27
  807.3 6.4 copy-start.29
  807.3 109.1 %copy-start.10 = (f32[1152]{0:T(1024)S(1)}, f32[1152]{0:T(1024)}, u32[]{:S(2)}) copy-start(f32[1152]{0:T(1024)} %copy-done.9) | copy-start | bytes 13828
  807.3 109.1 %copy-start.13 = (f32[512]{0:T(512)S(1)}, f32[512]{0:T(512)}, u32[]{:S(2)}) copy-start(f32[512]{0:T(512)} %copy-done.12) | copy-start | bytes 6148
  807.3 109.0 %copy-start.16 = (f32[512]{0:T(512)S(1)}, f32[512]{0:T(512)}, u32[]{:S(2)}) copy-start(f32[512]{0:T(512)} %copy-done.15) | copy-start | bytes 6148
  860.4 103.8 %copy-start.5 = (f32[512,1152]{1,0:T(8,128)S(1)}, f32[512,1152]{1,0:T(8,128)}, u32[]{:S(2)}) copy-start(f32[512,1152]{1,0:T(8,128)} %copy-done.4) | copy-start | bytes 7077892
  916.4 4.2 copy-start.23
  (23 other events, 47.4 us)
Sparse Core Ops, SparseCore 0:
  9.6 36.7 all-gather.11
  147.6 54.8 all-gather.9
  252.5 56.9 reduce-scatter.12
  311.0 33.9 all-gather.17
  346.7 56.0 all-gather.19
  404.3 33.9 all-gather.15
  440.7 56.0 all-gather.13
  526.4 56.9 reduce-scatter.16
  586.4 56.9 reduce-scatter.14
  651.0 56.8 all-gather.21
  710.3 38.0 reduce-scatter.24
  750.5 37.2 reduce-scatter.22
  790.1 31.4 reduce-scatter.20
  823.7 34.3 reduce-scatter.26
  861.0 55.2 reduce-scatter.18
where the time goes:
time: 980 us; the launch traced here: 974 us
  waiting for transfers between devices  464 us (47%)
  blocking collectives  221 us (23%)
  matrix products  155 us (16%)
  local copies, waits for them, and re-layouts  75 us (8%)
  other arithmetic  43 us (4%)
  between operations  14.5 us (1%)
    all_gather x1, blocking collectives, body(): lax.all_gather(norm_gains, ('dp', 'tensor'), axis=1, tiled=True)  71.1 us
    all_gather x1, blocking collectives, body(): lax.all_gather(row_biases, ('dp', 'tensor'), axis=1, tiled=True)  63.9 us
    all_gather x1, waiting for transfers between devices, body(): lax.all_gather(second_f.astype(jnp.bfloat16), 'tensor', axis=0, tiled=True)  58.5 us
    all_gather x1, waiting for transfers between devices, body(): lax.all_gather(cotangent, 'tensor', axis=0, tiled=True)  57.8 us
    reduce_scatter x1, waiting for transfers between devices, body(): lax.psum_scatter(jnp.dot(act_in, fc2_full, preferred_element_type=jnp.flo...  55.7 us
    reduce_scatter x1, waiting for transfers between devices, body(): lax.psum_scatter(jnp.dot(mixed, out_full, preferred_element_type=jnp.floa...  55.1 us
    reduce_scatter x1, waiting for transfers between devices, body(): lax.psum_scatter(jnp.einsum('irk,idk->rd', grad_proj, qkv_full, preferred...  51.7 us
    reduce_scatter x1, waiting for transfers between devices, body(): lax.psum_scatter(jnp.dot(grad_pre_in, fc1_full.T, preferred_element_type=...  43.9 us
  transfers between devices with their start and end apart: 15, of which 11 were waited for; matrix products, arithmetic and copies ran while one was open for 18% of the time, Pallas kernels for 0%

commit v1 on v0

--- a/solution.py
+++ b/solution.py
@@ -1,3 +1,4 @@
+import functools
 import jax
 import jax.numpy as jnp
 from jax import lax
@@ -6,6 +7,33 @@
 HD = 72
 SEQ = 256
 EPS = 1e-06
+
+
+def tails_apply(v0, dim_i):
+    last = list(v0.shape[1:])
+    last[dim_i] *= v0.shape[0]
+    return jnp.moveaxis(v0, 0, dim_i).reshape(last)
+
+
+def draft_tails(tile_in, which_axis, d_out):
+    axis_n = lax.axis_size(which_axis)
+    log = [(i0, (i0 + 1) % axis_n) for i0 in range(axis_n)]
+    panels = [(m, jj) for jj, m in log]
+    r_now, t_next = ([], [])
+    for dev in range(axis_n - 1):
+        if dev % 2 == 0:
+            r_now.append(lax.ppermute(r_now[-1] if r_now else tile_in, which_axis, perm=log))
+        else:
+            t_next.append(
+                lax.ppermute(t_next[-1] if t_next else tile_in, axis_name=which_axis, perm=panels)
+            )
+    u1 = jnp.stack([*r_now[::-1], tile_in, *t_next], axis=0)
+    clean = lax.axis_index(which_axis) - len(r_now)
+    u1 = u1[(jnp.arange(axis_n) - clean) % axis_n]
+    return tails_apply(u1, d_out)
+
+
+write_column = functools.partial(draft_tails, which_axis="tensor", d_out=0)
 
 
 def norm_rows(values, gain_row, shifts):
@@ -83,7 +111,7 @@
     first_f, normed_one, spread_one = norm_rows(inputs_f, gain_rows[0], shifts[0])
     first_in, cot_all = (
         lax.all_gather(first_f.astype(jnp.bfloat16), "tensor", axis=0, tiled=True),
-        lax.all_gather(cotangent, "tensor", axis=0, tiled=True),
+        write_column(cotangent),
     )
     group_rows = first_in.shape[0]
     images = group_rows // SEQ

time: 980 us -> 948 us (0.967)
  waiting for transfers between devices: 464 us -> 420 us
    ppermute x0 -> x3, waiting for transfers between devices: none -> 104 us  [the longest x2 67.6 us: draft_tails(): lax.ppermute(r_now[-1] if r_now else tile_in, which_axis, perm=log)]
    all_gather x1, waiting for transfers between devices: 58.5 us -> 0.01 us  [body(): lax.all_gather(second_f.astype(jnp.bfloat16), 'tensor', axis=0, tiled=True)]
    all_gather x1 -> x0, waiting for transfers between devices: 57.8 us -> none  [body(): lax.all_gather(cotangent, 'tensor', axis=0, tiled=True)]
    all_gather x1, waiting for transfers between devices: 24.8 us -> 0.01 us  [body(): lax.all_gather(w_fc1, 'dp', axis=0, tiled=True)]
  transfers between devices with their start and end apart: 15 -> 17, of which waited for: 11 -> 11; matrix products, arithmetic and copies ran while one was open for 18% -> 20% of each run, Pallas kernels for 0% -> 0%
where the time goes in v1:
time: 948 us; the launch traced here: 943 us
  waiting for transfers between devices  420 us (44%)
  blocking collectives  221 us (23%)
  matrix products  154 us (16%)
  local copies, waits for them, and re-layouts  80.7 us (9%)
  other arithmetic  47.7 us (5%)
  between operations  14.5 us (2%)
    all_gather x1, blocking collectives, body(): lax.all_gather(norm_gains, ('dp', 'tensor'), axis=1, tiled=True)  71.1 us
    ppermute x2, waiting for transfers between devices, draft_tails(): lax.ppermute(r_now[-1] if r_now else tile_in, which_axis, perm=log)  67.6 us
    all_gather x1, blocking collectives, body(): lax.all_gather(row_biases, ('dp', 'tensor'), axis=1, tiled=True)  63.9 us
    reduce_scatter x1, waiting for transfers between devices, body(): lax.psum_scatter(jnp.dot(mixed, out_full, preferred_element_type=jnp.floa...  56.3 us
    reduce_scatter x1, waiting for transfers between devices, body(): lax.psum_scatter(jnp.dot(act_in, fc2_full, preferred_element_type=jnp.flo...  55.6 us
    reduce_scatter x1, waiting for transfers between devices, body(): lax.psum_scatter(jnp.einsum('irk,idk->rd', grad_proj, qkv_full, preferred...  51.9 us
    reduce_scatter x1, waiting for transfers between devices, body(): lax.psum_scatter(jnp.dot(grad_pre_in, fc1_full.T, preferred_element_type=...  43 us
    unnamed x1, blocking collectives  40.3 us
  transfers between devices with their start and end apart: 17, of which 11 were waited for; matrix products, arithmetic and copies ran while one was open for 20% of the time, Pallas kernels for 0%

profile of v1, /device:TPU:0, one launch (start us, length us, event | category | flops | bytes accessed | tf_op | source)
XLA Modules:
  0.0 942.9 jit_solution(15672947329592630429)
XLA Ops:
  8.0 71.1 %all-gather = f32[32,36,2]{1,2,0:T(2,128)S(1)} all-gather(f32[1,36,2]{1,2,0:T(2,128)} %bitcast.190), channel_id=1, replica_groups=mesh['dp'=8,'tensor'=4] {'dp','tensor'}, dimensions={0}, use_global_device_ids=true | all-gather | bytes 9504 | tf_op jit(solution)/shard_map/all_gather | solution.py:101
  79.2 63.9 %all-gather.1 = f32[32,36,4]{1,2,0:T(4,128)S(1)} all-gather(f32[1,36,4]{1,2,0:T(4,128)} %bitcast.189), channel_id=1, replica_groups=mesh['dp'=8,'tensor'=4] {'dp','tensor'}, dimensions={0}, use_global_device_ids=true | all-gather | bytes 19008 | tf_op jit(solution)/shard_map/all_gather | solution.py:102
  148.2 16.7 %all_gather.31 = bf16[288,1152]{0,1:T(8,128)(2,1)} all-gather(bf16[288,144]{0,1:T(8,128)(2,1)S(1)} %copy-done.11), channel_id=1, replica_groups=mesh['dp'=8,'tensor'=4] {'dp'}, dimensions={1}, use_global_device_ids=true | all-gather | bytes 746496 | tf_op jit(solution)/shard_map/all_gather | solution.py:106
  164.8 37.7 %all-gather.9.cloned.1.call-done = bf16[2048,1152]{1,0:T(8,128)(2,1)} async-done(((bf16[512,1152]{1,0:T(8,128)(2,1)}), bf16[2048,1152]{1,0:T(8,128)(2,1)}) %all-gather.9.cloned.1.call-update) | async-done | bytes 4718608 | tf_op jit(solution)/shard_map/all_gather | solution.py:113
  208.6 5.3 fusion.56
  226.1 15.5 %while.26 = (s32[]{:T(128)}, bf16[4,2,256,4,72]{2,1,0,4,3:T(2,128)(2,1)}, f32[4,2,4,256]{3,2,1,0:T(4,128)}, bf16[4,2,256,4,72]{2,4,3,1,0:T(8,128)(2,1)}, bf16[4,...) while((s32[]{:T(128)}, bf16[4,2,256,4,72]{2,1,0,4,3:T(2,128)(2,1)}, ...), condition=%wide.region_5.6_spmd, body=%wide.region_2.5_spmd.sunk | while | flops 153761792 | bytes 8127585 | solution.py:138
  245.8 6.5 convolution_convert_fusion.5
  253.2 56.3 %reduce-scatter.13.cloned.1.call-done = bf16[512,1152]{1,0:T(8,128)(2,1)} async-done(((bf16[2048,1152]{1,0:T(8,128)(2,1)}), bf16[512,1152]{1,0:T(8,128)(2,1)}) %reduce-scatter.13.cloned.1.call-update) | async-done | bytes 1179664 | tf_op jit(solution)/shard_map/reduce_scatter | solution.py:140
  317.4 27.0 %collective-permute-done = bf16[512,1152]{1,0:T(8,128)(2,1)} collective-permute-done((bf16[512,1152]{1,0:T(8,128)(2,1)}, bf16[512,1152]{1,0:T(8,128)(2,1)}, u32[]{:S(2)}, u32[]{:S(2)}) %collective-permute-start) | collective-permute-done | bytes 1179680 | tf_op jit(solution)/shard_map/ppermute | solution.py:25
  345.6 36.6 %collective-permute-done.2 = bf16[512,1152]{1,0:T(8,128)(2,1)} collective-permute-done((bf16[512,1152]{1,0:T(8,128)(2,1)}, bf16[512,1152]{1,0:T(8,128)(2,1)}, u32[]{:S(2)}, u32[]{:S(2)}) %collective-permute-start.2) | collective-permute-done | bytes 1179680 | tf_op jit(solution)/shard_map/ppermute | solution.py:28
  382.2 40.6 %collective-permute-done.1 = bf16[512,1152]{1,0:T(8,128)(2,1)} collective-permute-done((bf16[512,1152]{1,0:T(8,128)(2,1)}, bf16[512,1152]{1,0:T(8,128)(2,1)}, u32[]{:S(2)}, u32[]{:S(2)}) %collective-permute-start.1) | collective-permute-done | bytes 1179680 | tf_op jit(solution)/shard_map/ppermute | solution.py:25
  427.0 5.7 gather_fusion
  432.7 10.7 %convolution_add_fusion = f32[2048,1076]{0,1:T(8,128)} fusion(bf16[2048,1152]{1,0:T(8,128)(2,1)} %all-gather.13.cloned.1.call-done, bf16[1152,1076]{1,0:T(8,128)(2,1)} %all-gather.15.cloned.1.call-done, f32[1076]{0:T(1024)} %param.21), kind=kOutput, calls=%fused_computation.50 | convolution fusion | flops 5079408640 | bytes 16016592 | tf_op jit(solution)/shard_map/dot_general | solution.py:149
  443.4 23.9 %all-gather.17.cloned.1.call-done = bf16[1076,1152]{0,1:T(8,128)(2,1)} async-done(((bf16[1076,144]{0,1:T(8,128)(2,1)}), bf16[1076,1152]{0,1:T(8,128)(2,1)}) %all-gather.17.cloned.1.call-update) | async-done | bytes 2479120 | tf_op jit(solution)/shard_map/all_gather | solution.py:108
  467.3 17.0 %fusion.76 = (f32[1076]{0:T(1024)}, bf16[2048,1076]{0,1:T(8,128)(2,1)S(1)}) fusion(f32[2048,1076]{0,1:T(8,128)} %convolution_add_fusion, bf16[2048,1152]{1,0:T(8,128)(2,1)} %bitcast.184, bf16[1076,1152]{0,1:T(8,128)(2,1)} %all-gather.17.cloned.1.call-done), kind=kOutput, calls=%fused_computation.151 | convolution fusion | flops 5123480576 | bytes 20423888 | tf_op jit(solution)/shard_map/dot_general | solution.py:161
  486.4 9.1 convolution_convert_fusion.3
  495.6 13.1 %convolution_convert_fusion.4 = bf16[2048,1152]{1,0:T(8,128)(2,1)} fusion(bf16[1076,1152]{0,1:T(8,128)(2,1)} %all-gather.17.cloned.1.call-done, f32[2048,1076]{0,1:T(8,128)} %convolution_add_fusion), kind=kOutput, calls=%fused_computation.61 | convolution fusion | flops 5099397120 | bytes 16012288 | tf_op jit(solution)/shard_map/dot_general | solution.py:153
  508.8 43.0 %reduce-scatter.17.cloned.1.call-done = bf16[512,1152]{1,0:T(8,128)(2,1)} async-done(((bf16[2048,1152]{1,0:T(8,128)(2,1)}), bf16[512,1152]{1,0:T(8,128)(2,1)}) %reduce-scatter.17.cloned.1.call-update) | async-done | bytes 1179664 | tf_op jit(solution)/shard_map/reduce_scatter | solution.py:166
  556.2 55.6 %reduce-scatter.15.cloned.1.call-done = bf16[512,1152]{1,0:T(8,128)(2,1)} async-done(((bf16[2048,1152]{1,0:T(8,128)(2,1)}), bf16[512,1152]{1,0:T(8,128)(2,1)}) %reduce-scatter.15.cloned.1.call-update) | async-done | bytes 1179664 | tf_op jit(solution)/shard_map/reduce_scatter | solution.py:152
  619.5 13.0 %convolution_convert_fusion.1 = bf16[1076,1152]{0,1:T(8,128)(2,1)} fusion(bf16[2048,1152]{1,0:T(8,128)(2,1)} %bitcast.185, f32[2048,1076]{0,1:T(8,128)} %convolution_add_fusion), kind=kOutput, calls=%fused_computation.58 | convolution fusion | flops 5098277376 | bytes 16012288 | tf_op jit(solution)/shard_map/dot_general | solution.py:160
  632.8 11.6 %convolution_convert_fusion.2 = bf16[1152,1076]{1,0:T(8,128)(2,1)} fusion(bf16[2048,1152]{1,0:T(8,128)(2,1)} %all-gather.13.cloned.1.call-done, bf16[2048,1076]{0,1:T(8,128)(2,1)} %copy-done.33), kind=kOutput, calls=%fused_computation.59 | convolution fusion | flops 5078444544 | bytes 11604992 | tf_op jit(solution)/shard_map/dot_general | solution.py:165
  644.5 31.9 %all-gather.19.cloned.1.call-done = bf16[2048,1152]{1,0:T(8,128)(2,1)} async-done(((bf16[512,1152]{1,0:T(8,128)(2,1)}), bf16[2048,1152]{1,0:T(8,128)(2,1)}) %all-gather.19.cloned.1.call-update) | async-done | bytes 4718608 | tf_op jit(solution)/shard_map/all_gather | solution.py:178
  685.8 29.5 %while.27 = (s32[]{:T(128)}, f32[4,2,256,4,72]{2,4,3,1,0:T(8,128)}, bf16[4,2,256,4,72]{2,4,3,1,0:T(8,128)(2,1)}, f32[4,2,256,4,72]{2,4,3,1,0:T(8,128)}, bf16[4,2...) while((s32[]{:T(128)}, f32[4,2,256,4,72]{2,4,3,1,0:T(8,128)}, ...), condition=%wide.region_15.16_spmd, body=%wide.region_13.15_spmd.sunk | while | flops 381302784 | bytes 29633716 | solution.py:183
  715.3 6.0 fusion.80
  731.3 6.4 convolution_convert_fusion.6
  743.9 8.2 fusion.48
  757.0 7.4 reshape.187
  764.6 11.0 %bitcast_convert_fusion = bf16[2048,1152]{1,0:T(8,128)(2,1)} fusion(bf16[3,2048,288]{1,2,0:T(8,128)(2,1)} %constant_dynamic-update-slice_fusion, bf16[3,1152,288]{2,1,0:T(8,128)(2,1)} %all-gather.11.cloned.1.call-done), kind=kOutput, calls=%fused_computation.49 | convolution fusion | flops 4079222784 | bytes 10248192 | tf_op jit(solution)/shard_map/irk,idk->rd/dot_general | solution.py:193
  782.0 28.7 %all-reduce.3 = (f32[2,288]{1,0:T(2,128)}, f32[1076]{0:T(1024)}) all-reduce(f32[2,288]{1,0:T(2,128)S(1)} %pad_maximum_fusion.3, f32[1076]{0:T(1024)S(1)} %copy-done.29), channel_id=1, replica_groups=mesh['dp'=8,'tensor'=4] {'dp'}, use_global_device_ids=true, to_apply=%region_30.31 | all-reduce | flops 1652 | bytes 13216 | tf_op jit(solution)/shard_map/psum | solution.py:203
  812.3 14.2 %reduce-scatter.27.cloned.1.call-done = bf16[144,864]{1,0:T(8,128)(2,1)} async-done(((bf16[1152,864]{1,0:T(8,128)(2,1)}), bf16[144,864]{1,0:T(8,128)(2,1)}) %reduce-scatter.27.cloned.1.call-update) | async-done | bytes 248848
  832.9 51.9 %reduce-scatter.19.cloned.1.call-done = bf16[512,1152]{1,0:T(8,128)(2,1)} async-done(((bf16[2048,1152]{1,0:T(8,128)(2,1)}), bf16[512,1152]{1,0:T(8,128)(2,1)}) %reduce-scatter.19.cloned.1.call-update) | async-done | bytes 1179664 | tf_op jit(solution)/shard_map/reduce_scatter | solution.py:192
  889.7 40.3 %all-reduce.2 = (f32[2,1152]{1,0:T(2,128)}, f32[4,1152]{1,0:T(4,128)}) all-reduce(f32[2,1152]{1,0:T(2,128)} %pad_maximum_fusion.2, f32[4,1152]{1,0:T(4,128)} %pad_maximum_fusion.1), channel_id=6, replica_groups=mesh['dp'=8,'tensor'=4] {'dp','tensor'}, use_global_device_ids=true, to_apply=%region_21.22.clone | all-reduce | flops 6912 | bytes 55296
  (243 shorter events, 157.5 us)
Async XLA Ops:
  7.2 138.3 %copy-start = (bf16[512,1152]{1,0:T(8,128)(2,1)S(1)}, bf16[512,1152]{1,0:T(8,128)(2,1)}, u32[]{:S(2)}) copy-start(bf16[512,1152]{1,0:T(8,128)(2,1)} %param.14) | copy-start | bytes 3538948
  7.2 157.7 %all-gather.11.cloned.1.call-start = ((), (), s32[]{:S(2)}) async-start(), calls=%async_computation.9 | async-start | bytes 2985984 | tf_op jit(solution)/shard_map/all_gather | solution.py:105
  7.9 194.6 %all-gather.9.cloned.1.call-start = ((), (), s32[]{:S(2)}) async-start(), calls=%async_computation.8 | async-start | bytes 5898240 | tf_op jit(solution)/shard_map/all_gather | solution.py:113
  145.9 56.6 %copy-start.15 = (f32[512]{0:T(512)}, f32[512]{0:T(512)S(1)}, u32[]{:S(2)}) copy-start(f32[512]{0:T(512)S(1)} %add_rsqrt_fusion.1) | copy-start | bytes 6148
  147.5 162.0 %reduce-scatter.13.cloned.1.call-start = ((), (), s32[]{:S(2)}) async-start(), calls=%async_computation.10 | async-start | bytes 5898240 | tf_op jit(solution)/shard_map/reduce_scatter | solution.py:140
  241.6 10.7 %copy-start.2 = (bf16[4,2,256,4,72]{2,4,3,1,0:T(8,128)(2,1)}, bf16[4,2,256,4,72]{2,4,3,1,0:T(8,128)(2,1)S(1)}, u32[]{:S(2)}) copy-start(bf16[4,2,256,4,72]{2,4,3,1,0:T(8,128)(2,1)S(1)} %get-tuple-element.413) | copy-start | bytes 3538948
  252.4 180.3 %all-gather.15.cloned.1.call-start = ((), (), s32[]{:S(2)}) async-start(), calls=%async_computation.12 | async-start | bytes 2985984 | tf_op jit(solution)/shard_map/all_gather | solution.py:107
  252.9 179.8 %all-gather.13.cloned.1.call-start = ((), (), s32[]{:S(2)}) async-start(), calls=%async_computation.11 | async-start | bytes 5898240 | tf_op jit(solution)/shard_map/all_gather | solution.py:148
  314.3 153.0 %all-gather.17.cloned.1.call-start = ((), (), s32[]{:S(2)}) async-start(), calls=%async_computation.13 | async-start | bytes 2985984 | tf_op jit(solution)/shard_map/all_gather | solution.py:108
  314.3 30.1 %collective-permute-start = (bf16[512,1152]{1,0:T(8,128)(2,1)}, bf16[512,1152]{1,0:T(8,128)(2,1)}, u32[]{:S(2)}, u32[]{:S(2)}) collective-permute-start(bf16[512,1152]{1,0:T(8,128)(2,1)} %param.23), channel_id=1, source_target_pairs={{0,1},{1,2},{2,3},{3,0},{4,5},{5,6},{6,7},{7,4},{8,9},{9,10},{10,1... | collective-permute-start | bytes 3538952 | tf_op jit(solution)/shard_map/ppermute | solution.py:25
  315.9 235.9 %reduce-scatter.17.cloned.1.call-start = ((), (), s32[]{:S(2)}) async-start(), calls=%async_computation.15 | async-start | bytes 5898240 | tf_op jit(solution)/shard_map/reduce_scatter | solution.py:166
  315.9 66.3 %collective-permute-start.2 = (bf16[512,1152]{1,0:T(8,128)(2,1)}, bf16[512,1152]{1,0:T(8,128)(2,1)}, u32[]{:S(2)}, u32[]{:S(2)}) collective-permute-start(bf16[512,1152]{1,0:T(8,128)(2,1)} %param.23), channel_id=1, source_target_pairs={{1,0},{2,1},{3,2},{0,3},{5,4},{6,5},{7,6},{4,7},{9,8},{10,9},{11,1... | collective-permute-start | bytes 3538952 | tf_op jit(solution)/shard_map/ppermute | solution.py:28
  344.4 78.5 %collective-permute-start.1 = (bf16[512,1152]{1,0:T(8,128)(2,1)}, bf16[512,1152]{1,0:T(8,128)(2,1)}, u32[]{:S(2)}, u32[]{:S(2)}) collective-permute-start(bf16[512,1152]{1,0:T(8,128)(2,1)} %collective-permute-done), channel_id=1, source_target_pairs={{0,1},{1,2},{2,3},{3,0},{4,5},{5,6},{6,7},{7,4},{8,9},{9,10},{10,1... | collective-permute-start | bytes 3538952 | tf_op jit(solution)/shard_map/ppermute | solution.py:25
  467.3 19.1 %copy-start.32 = (bf16[1152,1076]{1,0:T(8,128)(2,1)S(1)}, bf16[1152,1076]{1,0:T(8,128)(2,1)}, u32[]{:S(2)}) copy-start(bf16[1152,1076]{1,0:T(8,128)(2,1)} %all-gather.15.cloned.1.call-done) | copy-start | bytes 7437316
  495.5 116.2 %reduce-scatter.15.cloned.1.call-start = ((), (), s32[]{:S(2)}) async-start(), calls=%async_computation.14 | async-start | bytes 5898240 | tf_op jit(solution)/shard_map/reduce_scatter | solution.py:152
  508.7 167.6 %all-gather.19.cloned.1.call-start = ((), (), s32[]{:S(2)}) async-start(), calls=%async_computation.16 | async-start | bytes 5898240 | tf_op jit(solution)/shard_map/all_gather | solution.py:178
  619.2 156.5 %reduce-scatter.25.cloned.1.call-start = ((), (), s32[]{:S(2)}) async-start(), calls=%async_computation.20 | async-start | bytes 2985984 | tf_op jit(solution)/shard_map/reduce_scatter | solution.py:214
  632.5 145.1 %reduce-scatter.23.cloned.1.call-start = ((), (), s32[]{:S(2)}) async-start(), calls=%async_computation.19 | async-start | bytes 2985984 | tf_op jit(solution)/shard_map/reduce_scatter | solution.py:211
  644.4 32.0 %copy-start.8 = (bf16[288,1152]{0,1:T(8,128)(2,1)S(1)}, bf16[288,1152]{0,1:T(8,128)(2,1)}, u32[]{:S(2)}) copy-start(bf16[288,1152]{0,1:T(8,128)(2,1)} %all_gather.31) | copy-start | bytes 1990660
  644.4 166.3 %reduce-scatter.21.cloned.1.call-start = ((), (), s32[]{:S(2)}) async-start(), calls=%async_computation.18 | async-start | bytes 995328 | tf_op jit(solution)/shard_map/reduce_scatter | solution.py:208
  737.8 88.7 %reduce-scatter.27.cloned.1.call-start = ((), (), s32[]{:S(2)}) async-start(), calls=%async_computation.21 | async-start | bytes 2322432
  764.5 120.4 %reduce-scatter.19.cloned.1.call-start = ((), (), s32[]{:S(2)}) async-start(), calls=%async_computation.17 | async-start | bytes 5898240 | tf_op jit(solution)/shard_map/reduce_scatter | solution.py:192
  775.6 4.5 copy-start.18
  775.6 5.1 copy-start.22
  775.6 5.6 copy-start.21
  775.6 6.2 copy-start.28
  775.6 6.3 copy-start.27
  775.6 6.4 copy-start.29
  775.6 109.2 %copy-start.10 = (f32[1152]{0:T(1024)S(1)}, f32[1152]{0:T(1024)}, u32[]{:S(2)}) copy-start(f32[1152]{0:T(1024)} %copy-done.9) | copy-start | bytes 13828
  775.7 109.2 %copy-start.13 = (f32[512]{0:T(512)S(1)}, f32[512]{0:T(512)}, u32[]{:S(2)}) copy-start(f32[512]{0:T(512)} %copy-done.12) | copy-start | bytes 6148
  775.7 109.2 %copy-start.16 = (f32[512]{0:T(512)S(1)}, f32[512]{0:T(512)}, u32[]{:S(2)}) copy-start(f32[512]{0:T(512)} %copy-done.15) | copy-start | bytes 6148
  828.7 104.0 %copy-start.5 = (f32[512,1152]{1,0:T(8,128)S(1)}, f32[512,1152]{1,0:T(8,128)}, u32[]{:S(2)}) copy-start(f32[512,1152]{1,0:T(8,128)} %copy-done.4) | copy-start | bytes 7077892
  (25 other events, 56.0 us)
Sparse Core Ops, SparseCore 0:
  9.6 36.7 all-gather.10
  147.6 54.8 all-gather.8
  252.5 56.9 reduce-scatter.12
  311.0 33.9 all-gather.14
  347.2 84.5 all-gather.12
  433.3 33.9 all-gather.16
  495.7 56.0 reduce-scatter.16
  554.8 56.9 reduce-scatter.14
  619.4 56.9 all-gather.18
  678.5 38.0 reduce-scatter.24
  718.9 37.3 reduce-scatter.22
  758.4 31.2 reduce-scatter.20
  792.0 34.4 reduce-scatter.26
  829.3 55.4 reduce-scatter.18
